TPU v7x, 32 devices: a whole 2x2x4 slice. The times are simulated.
32 devices in a mesh: groups: 2 (over y), seq: 8 (over z, x), tensor: 2 (over core).
Axes of the slice: x: 2, y: 2, z: 4, core: 2. Of those that a mesh axis runs over, the one named last changes fastest.
Arguments:
- queries: bfloat16 [2048, 1536], P(('groups', 'seq'), 'tensor'), parts along dimension 0, may hold values from -64 to 64
- keys: bfloat16 [2048, 1536], P(('groups', 'seq'), 'tensor'), parts along dimension 0, may hold values from -6 to 6
- values: bfloat16 [2048, 1536], P(('groups', 'seq'), 'tensor'), parts along dimension 0, may hold values from -6 to 6
- text_keys: bfloat16 [64, 1536], P(('groups', 'seq'), 'tensor'), parts along dimension 0, may hold values from -6 to 6
- text_values: bfloat16 [64, 1536], P(('groups', 'seq'), 'tensor'), parts along dimension 0, may hold values from -6 to 6
- conv_weight: bfloat16 [4, 1536], P(None, 'tensor'), may hold values from -3 to 3
- out_weight: bfloat16 [1536, 1536], P('tensor'), may hold values from -0.15625 to 0.15625
- image_hidden: bfloat16 [2048, 1536], P(('groups', 'seq')), parts along dimension 0, may hold values from -6 to 6
- gate: bfloat16 [3072], P('groups'), parts along dimension 0, may hold values from -8 to 8
Outputs:
- mixed: bfloat16 [2048, 1536], P(('groups', 'seq')), parts along dimension 0
There are 2 independent parts, one for each index of `groups`. A program takes and returns all parts, laid end to end along the dimension named above; an argument that names none is the same for every part. Nothing has to cross between parts.
All inputs are finite; a program needn't handle non-finite values.
Results may differ from a plain program's by a relative error of at most 0.011.
Values may be sent and summed in bfloat16 or wider, within the bound.
A program may use at most 64 MiB of HBM per device.

v0:
```python
import math

import jax
import jax.numpy as jnp
from jax import lax
from jax.sharding import PartitionSpec as P

HEAD_DIM = 128


key_block = 512


def rope_angles(row_pos, col_pos, head_dim):
    lead_dims = head_dim // 8
    group_dims = head_dim * 7 // 16
    frequency = 10000.0 ** (-(2.0 * jnp.arange(group_dims // 2, dtype=jnp.float32)) / group_dims)
    zero_angles = jnp.zeros((row_pos.shape[0], lead_dims // 2), jnp.float32)
    return jnp.concatenate(
        [zero_angles, row_pos[:, None] * frequency[None, :], col_pos[:, None] * frequency[None, :]],
        axis=1,
    )


def apply_rope(field, angles):
    paired = field.reshape(field.shape[0], field.shape[1], field.shape[2] // 2, 2)
    even_part = paired[..., 0]
    odd_part = paired[..., 1]
    cos_part = jnp.cos(angles)[:, None, :]
    sin_part = jnp.sin(angles)[:, None, :]
    turned = jnp.stack(
        [even_part * cos_part - odd_part * sin_part, even_part * sin_part + odd_part * cos_part],
        axis=-1,
    )
    return turned.reshape(field.shape)


def compress(field, taps, row_width):
    features = field.shape[1]
    grid_cells = field.astype(jnp.float32).reshape(2, row_width // 2, 2, features)
    tap_grid = taps.astype(jnp.float32).reshape(2, 2, features)
    return (
        grid_cells[0, :, 0] * tap_grid[0, 0]
        + grid_cells[0, :, 1] * tap_grid[0, 1]
        + grid_cells[1, :, 0] * tap_grid[1, 0]
        + grid_cells[1, :, 1] * tap_grid[1, 1]
    )


def absorb_block(carry, key_rows, value_rows, queries_rot):
    row_max, row_total, accumulated = carry
    heads_dev = queries_rot.shape[1]
    key_heads = key_rows.reshape(key_rows.shape[0], heads_dev, -1)
    value_heads = value_rows.reshape(value_rows.shape[0], heads_dev, -1)
    scores = jnp.einsum(
        "qhd,khd->hqk", queries_rot, key_heads, preferred_element_type=jnp.float32
    ) * (1.0 / math.sqrt(HEAD_DIM))
    new_max = jnp.maximum(row_max, jnp.max(scores, axis=-1))
    rescale = jnp.exp(row_max - new_max)
    weights = jnp.exp(scores - new_max[:, :, None]).astype(jnp.bfloat16)
    row_total = row_total * rescale + jnp.sum(weights.astype(jnp.float32), axis=-1)
    mixed_values = jnp.einsum(
        "hqk,khd->qhd", weights, value_heads, preferred_element_type=jnp.float32
    )
    accumulated = accumulated * rescale.T[:, :, None] + mixed_values
    return (new_max, row_total, accumulated)


def absorb(carry, key_rows, value_rows, queries_rot):
    key_count = key_rows.shape[0]
    if key_count > key_block and key_count % key_block == 0:
        stacked_keys = key_rows.reshape(key_count // key_block, key_block, key_rows.shape[1])
        stacked_values = value_rows.reshape(key_count // key_block, key_block, value_rows.shape[1])

        def one_step(running, block_pair):
            return (absorb_block(running, block_pair[0], block_pair[1], queries_rot), None)

        carry, unused = lax.scan(one_step, carry, (stacked_keys, stacked_values))
        return carry
    return absorb_block(carry, key_rows, value_rows, queries_rot)


def local(
    queries, keys, values, text_keys, text_values, conv_weight, out_weight, image_hidden, gate
):
    local_tokens, features = queries.shape
    row_width = local_tokens // 2
    heads_dev = features // HEAD_DIM
    seq_place = lax.axis_index("seq").astype(jnp.float32)
    token_ids = jnp.arange(local_tokens, dtype=jnp.int32)
    query_rows = 2.0 * seq_place + (token_ids // row_width).astype(jnp.float32)
    query_cols = (token_ids % row_width).astype(jnp.float32)
    queries_rot = apply_rope(
        queries.astype(jnp.float32).reshape(local_tokens, heads_dev, HEAD_DIM),
        rope_angles(query_rows, query_cols, HEAD_DIM),
    ).astype(jnp.bfloat16)
    patch_ids = jnp.arange(row_width // 2, dtype=jnp.int32).astype(jnp.float32)
    patch_rows = 2.0 * seq_place + 0.5 + 0.0 * patch_ids
    patch_cols = 2.0 * patch_ids + 0.5
    short_keys = (
        apply_rope(
            compress(keys, conv_weight, row_width).reshape(row_width // 2, heads_dev, HEAD_DIM),
            rope_angles(patch_rows, patch_cols, HEAD_DIM),
        )
        .astype(jnp.bfloat16)
        .reshape(row_width // 2, features)
    )
    short_values = compress(values, conv_weight, row_width).astype(jnp.bfloat16)
    initial = (
        jnp.full((heads_dev, local_tokens), -1e30, jnp.float32),
        jnp.zeros((heads_dev, local_tokens), jnp.float32),
        jnp.zeros((local_tokens, heads_dev, HEAD_DIM), jnp.float32),
    )
    all_text_keys, all_text_values = (
        lax.all_gather(text_keys, "seq", axis=0, tiled=True),
        lax.all_gather(text_values, "seq", axis=0, tiled=True),
    )
    after_text = absorb(initial, all_text_keys, all_text_values, queries_rot)
    row_max, row_total, accumulated = absorb(
        after_text,
        lax.all_gather(short_keys, "seq", axis=0, tiled=True),
        lax.all_gather(short_values, "seq", axis=0, tiled=True),
        queries_rot,
    )
    attended = (
        (accumulated / row_total.T[:, :, None]).astype(jnp.bfloat16).reshape(local_tokens, features)
    )
    projected = lax.psum(
        jnp.dot(attended, out_weight, preferred_element_type=jnp.float32).astype(jnp.bfloat16),
        "tensor",
    ).astype(jnp.float32)
    return (
        image_hidden.astype(jnp.float32) + gate.astype(jnp.float32)[None, :] * projected
    ).astype(jnp.bfloat16)


def solution(mesh):
    placed = (
        P(("groups", "seq"), "tensor"),
        P(("groups", "seq"), "tensor"),
        P(("groups", "seq"), "tensor"),
        P(("groups", "seq"), "tensor"),
        P(("groups", "seq"), "tensor"),
        P(None, "tensor"),
        P("tensor", None),
        P(("groups", "seq"), None),
        P("groups"),
    )
    return jax.shard_map(
        local, mesh=mesh, in_specs=placed, out_specs=P(("groups", "seq"), None), check_vma=False
    )
```

profile of v0, /device:TPU:0, one launch (start us, length us, event | category | flops | bytes accessed | tf_op | source)
XLA Modules:
  0.0 191.8 jit_solution(10425235532652120512)
XLA Ops:
  6.5 0.5 multiply_power_fusion
  7.1 0.6 fusion.22
  7.6 0.7 reshape.261
  8.4 0.8 mul.304
  9.2 0.8 mul.307
  10.1 0.8 mul.310
  10.9 0.8 mul.313
  11.7 1.1 reshape.259
  12.9 1.0 fusion.27
  13.8 0.2 copy.66
  14.0 0.2 copy.63
  14.2 1.1 copy.64
  15.2 1.8 copy.65
  17.0 0.6 fusion.24
  17.6 0.7 broadcast_multiply_fusion.1
  18.3 0.2 fusion.15
  18.5 3.4 %multiply_add_fusion = f32[32,6,64,2]{0,3,2,1:T(2,128)S(1)} fusion(f32[32,6,64,2]{0,3,2,1:T(2,128)S(1)} %bitcast.86, f32[32,6,64,2]{0,3,2,1:T(2,128)} %bitcast.89, f32[32,6,64,2]{0,3,2,1:T(2,128)S(1)} %bitcast.88, f32[32,6,64,2]{0,3,2,1:T(2,128)S(1)} %bitcast.87, f32[6,64,2]{2,1,0:T(8,128)} %mul.313, f32[6,64,2]{2,1,0:T(8,128)} %mul.310, ...), kind=kLoop, calls=%fused_computation.13 | loop fusion | flops 172032 | bytes 503808 | tf_op jit(solution)/shard_map/add | solution.py:43
  21.9 0.0 copy-start.4
  22.0 0.5 subtract_convert_fusion
  22.5 0.5 pad_maximum_fusion.1
  23.0 0.1 copy.51
  23.1 32.8 %all_gather.14 = bf16[256,768]{1,0:T(8,128)(2,1)S(1)} all-gather(bf16[32,768]{1,0:T(8,128)(2,1)S(1)} %copy.51), channel_id=1, replica_groups=mesh['groups'=2,'seq'=8,'tensor'=2] {'seq'}, dimensions={0}, use_global_device_ids=true | all-gather | bytes 442368 | tf_op jit(solution)/shard_map/all_gather | solution.py:121
  55.9 0.2 copy.52
  56.1 0.2 copy.43
  56.2 0.1 convert.20
  56.4 31.0 %all-gather = bf16[8,4,768]{2,1,0:T(4,128)(2,1)S(1)} all-gather(bf16[1,4,768]{2,1,0:T(4,128)(2,1)} %bitcast.93), channel_id=1, replica_groups=mesh['groups'=2,'seq'=8,'tensor'=2] {'seq'}, dimensions={0}, use_global_device_ids=true | all-gather | bytes 55296 | tf_op jit(solution)/shard_map/all_gather | solution.py:115
  87.4 0.7 reshape.246
  88.0 0.8 broadcast_multiply_fusion.3
  88.8 0.8 fusion.17
  89.6 0.5 subtract_convert_fusion.1
  90.1 0.5 pad_maximum_fusion
  90.6 1.0 fusion.30
  91.5 1.4 fusion.29
  92.9 1.1 reshape.263
  94.1 0.3 fusion.28
  94.4 0.0 copy-start.5
  94.4 31.0 %all_gather.15 = bf16[256,768]{1,0:T(8,128)(2,1)S(1)} all-gather(bf16[32,768]{1,0:T(8,128)(2,1)S(1)} %fusion.8), channel_id=1, replica_groups=mesh['groups'=2,'seq'=8,'tensor'=2] {'seq'}, dimensions={0}, use_global_device_ids=true | all-gather | bytes 442368 | tf_op jit(solution)/shard_map/all_gather | solution.py:122
  125.4 0.9 copy.58
  126.3 0.7 broadcast_maximum_fusion
  127.0 0.3 convert_reduce_fusion
  127.3 2.1 %convolution_bitcast_fusion.1 = f32[128,6,128]{0,2,1:T(8,128)} fusion(bf16[256,6,128]{0,2,1:T(8,128)(2,1)} %bitcast.85, f32[6,128,256]{2,1,0:T(8,128)S(1)} %get-tuple-element.37, f32[6,128]{1,0:T(8,128)S(1)} %get-tuple-element.29), kind=kOutput, calls=%fused_computation.4 | convolution fusion | flops 50724864 | bytes 1575936 | tf_op jit(solution)/shard_map/hqk,khd->qhd/dot_general | solution.py:62
  129.4 30.8 %all-gather.1 = bf16[8,4,768]{2,1,0:T(4,128)(2,1)S(1)} all-gather(bf16[1,4,768]{2,1,0:T(4,128)(2,1)S(1)} %bitcast.94), channel_id=1, replica_groups=mesh['groups'=2,'seq'=8,'tensor'=2] {'seq'}, dimensions={0}, use_global_device_ids=true | all-gather | bytes 55296 | tf_op jit(solution)/shard_map/all_gather | solution.py:116
  160.3 0.7 bitcast_add_fusion
  161.0 1.4 fusion.4
  162.4 1.2 convolution_convert_fusion
  163.6 0.0 all-reduce.2.cloned.1.call-update
  163.7 19.4 %all-reduce.2.cloned.1.call-done = bf16[128,1536]{1,0:T(8,128)(2,1)} async-done(((bf16[128,1536]{1,0:T(8,128)(2,1)}), bf16[128,1536]{1,0:T(8,128)(2,1)}) %all-reduce.2.cloned.1.call-update) | async-done | bytes 393232 | tf_op jit(solution)/shard_map/psum | solution.py:128
  183.1 1.9 add_convert_fusion
  (23 shorter events, 0.2 us)
Async XLA Ops:
  6.5 155.8 %copy-start = (bf16[768,1536]{1,0:T(8,128)(2,1)S(1)}, bf16[768,1536]{1,0:T(8,128)(2,1)}, u32[]{:S(2)}) copy-start(bf16[768,1536]{1,0:T(8,128)(2,1)} %param.15) | copy-start | bytes 7077892
  6.5 176.6 %all-reduce.2.cloned.1.call-start = ((), (), s32[]{:S(2)}) async-start(), calls=%async_computation | async-start | bytes 786432 | tf_op jit(solution)/shard_map/psum | solution.py:128
  17.6 0.9 copy-start.7
  21.9 34.1 %copy-start.4 = (bf16[128,768]{1,0:T(8,128)(2,1)S(1)}, bf16[128,768]{1,0:T(8,128)(2,1)}, u32[]{:S(2)}) copy-start(bf16[128,768]{1,0:T(8,128)(2,1)} %param.9) | copy-start | bytes 589828
  88.0 3.5 %copy-start.3 = (bf16[32,6,128]{2,1,0:T(8,128)(2,1)S(1)}, bf16[32,6,128]{2,1,0:T(8,128)(2,1)}, u32[]{:S(2)}) copy-start(bf16[32,6,128]{2,1,0:T(8,128)(2,1)} %reshape.246) | copy-start | bytes 147460
  94.4 35.0 %copy-start.5 = (bf16[4,768]{1,0:T(4,128)(2,1)S(1)}, bf16[4,768]{1,0:T(4,128)(2,1)}, u32[]{:S(2)}) copy-start(bf16[4,768]{1,0:T(4,128)(2,1)} %param.13) | copy-start | bytes 18436
  126.3 33.9 %copy-start.2 = (f32[6,128,32]{1,2,0:T(8,128)S(1)}, f32[6,128,32]{1,2,0:T(8,128)}, u32[]{:S(2)}) copy-start(f32[6,128,32]{1,2,0:T(8,128)} %get-tuple-element.35) | copy-start | bytes 294916
  161.0 2.7 %copy-start.6 = (bf16[1536]{0:T(1024)(128)(2,1)S(1)}, bf16[1536]{0:T(1024)(128)(2,1)}, u32[]{:S(2)}) copy-start(bf16[1536]{0:T(1024)(128)(2,1)} %param.17) | copy-start | bytes 9220
  161.0 22.1 %copy-start.1 = (bf16[128,1536]{1,0:T(8,128)(2,1)S(1)}, bf16[128,1536]{1,0:T(8,128)(2,1)}, u32[]{:S(2)}) copy-start(bf16[128,1536]{1,0:T(8,128)(2,1)} %param.16) | copy-start | bytes 1179652
Sparse Core Ops, SparseCore 0:
  163.8 19.2 all-reduce.1
where the time goes:
time: 192 us
  blocking collectives  125 us (65%)
  waiting for transfers between devices  19.4 us (10%)
  between operations  13.6 us (7%)
  other arithmetic  13.3 us (7%)
  local copies, waits for them, and re-layouts  12.9 us (7%)
  matrix products  7.08 us (4%)
    all_gather x1, blocking collectives, local(): lax.all_gather(short_keys, 'seq', axis=0, tiled=True)  32.8 us
    all_gather x1, blocking collectives, local(): lax.all_gather(text_keys, 'seq', axis=0, tiled=True)  31 us
    all_gather x1, blocking collectives, local(): lax.all_gather(short_values, 'seq', axis=0, tiled=True)  31 us
    all_gather x1, blocking collectives, local(): lax.all_gather(text_values, 'seq', axis=0, tiled=True)  30.8 us
    psum x1, waiting for transfers between devices, local(): lax.psum(jnp.dot(attended, out_weight, preferred_element_type=jnp.float32...  19.4 us
  transfers between devices with their start and end apart: 1, of which 1 were waited for; matrix products, arithmetic and copies ran while one was open for 0% of the time, Pallas kernels for 0%

commit v1 on v0

v1 whole, which is shorter than its diff:
```python
import functools
import math

import jax
import jax.numpy as jnp
import numpy as np
from jax import lax
from jax.experimental import pallas as pl
from jax.experimental.pallas import tpu as pltpu
from jax.sharding import PartitionSpec as P

HEAD_DIM = 128
MESH = pl.DeviceIdType.MESH


def position_tables(places, row_width):
    lead = HEAD_DIM // 8
    group = HEAD_DIM * 7 // 16
    frequency = np.power(
        np.float32(10000.0), -(2.0 * np.arange(group // 2, dtype=np.float32)) / np.float32(group)
    ).astype(np.float32)
    pair_frequency = np.repeat(frequency, 2)
    sign = np.where(np.arange(group) % 2 == 0, -1.0, 1.0)

    def turned(positions):
        angles = (np.asarray(positions, np.float32)[:, None] * pair_frequency[None, :]).astype(np.float64)
        return np.cos(angles), np.sin(angles) * sign

    def row_part(positions):
        cos_part, sin_part = turned(positions)
        count = len(positions)
        full_cos = np.zeros((count, HEAD_DIM))
        full_sin = np.zeros((count, HEAD_DIM))
        full_cos[:, :lead] = 1.0
        full_cos[:, lead : lead + group] = cos_part
        full_sin[:, lead : lead + group] = sin_part
        return full_cos, full_sin

    def col_part(positions):
        cos_part, sin_part = turned(positions)
        count = len(positions)
        full_cos = np.zeros((count, HEAD_DIM))
        full_sin = np.zeros((count, HEAD_DIM))
        full_cos[:, lead + group :] = cos_part
        full_sin[:, lead + group :] = sin_part
        return full_cos, full_sin

    place = np.arange(places, dtype=np.float32)
    rows = np.zeros((places, 8, HEAD_DIM))
    rows[:, 0], rows[:, 2] = row_part(2.0 * place)
    rows[:, 1], rows[:, 3] = row_part(2.0 * place + 1.0)
    rows[:, 4], rows[:, 5] = row_part(2.0 * place + 0.5)
    cos_q, sin_q = col_part(np.arange(row_width))
    cos_k, sin_k = col_part(2.0 * np.arange(row_width // 2) + 0.5)
    cols = np.concatenate([cos_q, sin_q, cos_k, sin_k], axis=0)
    return rows.astype(np.float32), cols.astype(np.float32)


def fused(
    places, inner, queries, keys, values, text_keys, text_values, conv_weight, out_weight, image_hidden,
    gate, row_table, col_table, mixed, key_buf, value_buf, text_buf, text_all, query_in, key_in, value_in,
    weight_buf, hidden_buf, query_rot, attended, own_part, peer_part, load_sem, key_send, key_recv,
    value_send, value_recv, text_send, text_recv, part_send, part_recv,
):
    tokens, features = query_in.shape
    heads = features // HEAD_DIM
    row_width = tokens // 2
    patches = row_width // 2
    text_rows = text_buf.shape[2]
    outer = places // inner
    parts = own_part.shape[0]
    part_width = own_part.shape[2]
    me = lax.axis_index("seq")
    core = lax.axis_index("tensor")
    my_outer = me // inner
    my_inner = lax.rem(me, inner)

    loads = [
        pltpu.make_async_copy(keys, key_in, load_sem.at[0]),
        pltpu.make_async_copy(values, value_in, load_sem.at[1]),
        pltpu.make_async_copy(text_keys, text_buf.at[me, 0], load_sem.at[2]),
        pltpu.make_async_copy(text_values, text_buf.at[me, 1], load_sem.at[3]),
        pltpu.make_async_copy(queries, query_in, load_sem.at[4]),
        pltpu.make_async_copy(out_weight, weight_buf, load_sem.at[5]),
        pltpu.make_async_copy(image_hidden, hidden_buf, load_sem.at[6]),
    ]
    for load in loads:
        load.start()

    barrier = pltpu.get_barrier_semaphore()
    for step in range(1, places):
        pl.semaphore_signal(
            barrier, inc=1, device_id={"seq": lax.rem(me + step, places)}, device_id_type=MESH
        )
    pl.semaphore_signal(barrier, inc=1, device_id={"tensor": 1 - core}, device_id_type=MESH)

    row_of = lax.broadcasted_iota(jnp.int32, (tokens, tokens), 0)
    token_of = lax.broadcasted_iota(jnp.int32, (tokens, tokens), 1)
    tap_of = row_of // patches
    wanted = (tap_of // 2) * row_width + 2 * (row_of % patches) + tap_of % 2
    pick = (token_of == wanted).astype(jnp.bfloat16)
    taps = conv_weight[...].astype(jnp.float32)

    def compress(field):
        picked = jnp.dot(pick, field, preferred_element_type=jnp.float32)
        total = picked[:patches] * taps[0:1]
        for tap in range(1, 4):
            total = total + picked[tap * patches : (tap + 1) * patches] * taps[tap : tap + 1]
        return total

    my_rows = row_table[me]
    cos_k = my_rows[4:5] + col_table[2 * row_width : 2 * row_width + patches]
    sin_k = my_rows[5:6] + col_table[2 * row_width + patches : 2 * row_width + 2 * patches]
    even = lax.broadcasted_iota(jnp.int32, (patches, HEAD_DIM), 1) % 2 == 0
    loads[0].wait()
    short_raw = compress(key_in[...])
    for head in range(heads):
        lanes = slice(head * HEAD_DIM, (head + 1) * HEAD_DIM)
        raw = short_raw[:, lanes]
        swapped = jnp.where(even, pltpu.roll(raw, HEAD_DIM - 1, 1), pltpu.roll(raw, 1, 1))
        key_buf[me, :, lanes] = (raw * cos_k + swapped * sin_k).astype(jnp.bfloat16)
    loads[1].wait()
    value_buf[me] = compress(value_in[...]).astype(jnp.bfloat16)
    loads[2].wait()
    loads[3].wait()

    pl.semaphore_wait(barrier, places)

    sends = []

    def send(buf, slot, send_sem, recv_sem, at, target):
        copy = pltpu.make_async_remote_copy(
            src_ref=buf.at[slot],
            dst_ref=buf.at[slot],
            send_sem=send_sem.at[at],
            recv_sem=recv_sem.at[slot],
            device_id={"seq": target},
            device_id_type=MESH,
        )
        copy.start()
        sends.append(copy)

    def arrive(buf, slot, send_sem, recv_sem):
        pltpu.make_async_remote_copy(
            src_ref=buf.at[slot],
            dst_ref=buf.at[slot],
            send_sem=send_sem.at[0],
            recv_sem=recv_sem.at[slot],
            device_id={"seq": me},
            device_id_type=MESH,
        ).wait_recv()

    outer_peers = [lax.rem(my_outer + step, outer) for step in range(1, outer)]
    inner_peers = [lax.rem(my_inner + step, inner) for step in range(1, inner)]

    def send_own(buf, send_sem, recv_sem):
        at = 0
        for peer in outer_peers:
            send(buf, me, send_sem, recv_sem, at, peer * inner + my_inner)
            at += 1
        for peer in inner_peers:
            send(buf, me, send_sem, recv_sem, at, my_outer * inner + peer)
            at += 1

    def forward(buf, send_sem, recv_sem):
        at = outer - 1 + inner - 1
        for step in range(outer - 1, 0, -1):
            source = lax.rem(my_outer + step, outer) * inner + my_inner
            arrive(buf, source, send_sem, recv_sem)
            for peer in inner_peers:
                send(buf, source, send_sem, recv_sem, at, my_outer * inner + peer)
                at += 1

    def collect(buf, send_sem, recv_sem):
        for peer in inner_peers:
            for step in range(outer):
                source = lax.rem(my_outer + outer - step, outer) * inner + peer
                arrive(buf, source, send_sem, recv_sem)

    send_own(key_buf, key_send, key_recv)
    for step in range(1, places):
        send(text_buf, me, text_send, text_recv, step, lax.rem(me + step, places))
    send_own(value_buf, value_send, value_recv)

    loads[4].wait()
    first = lax.broadcasted_iota(jnp.int32, (HEAD_DIM, HEAD_DIM), 0)
    second = lax.broadcasted_iota(jnp.int32, (HEAD_DIM, HEAD_DIM), 1)
    swap = (first == second + 1 - 2 * (second % 2)).astype(jnp.bfloat16)
    col_cos = col_table[:row_width]
    col_sin = col_table[row_width : 2 * row_width]
    for row in range(2):
        cos_q = my_rows[row : row + 1] + col_cos
        sin_q = my_rows[2 + row : 3 + row] + col_sin
        rows = slice(row * row_width, (row + 1) * row_width)
        for head in range(heads):
            lanes = slice(head * HEAD_DIM, (head + 1) * HEAD_DIM)
            plain = query_in[rows, lanes]
            crossed = jnp.dot(plain, swap, preferred_element_type=jnp.float32)
            query_rot[rows, lanes] = (plain.astype(jnp.float32) * cos_q + crossed * sin_q).astype(jnp.bfloat16)

    forward(key_buf, key_send, key_recv)

    for step in range(1, places):
        arrive(text_buf, lax.rem(me + step, places), text_send, text_recv)
    for kind in range(2):
        for place in range(places):
            text_all[kind, place * text_rows : (place + 1) * text_rows, :] = text_buf[place, kind].astype(
                jnp.float32
            )

    collect(key_buf, key_send, key_recv)
    forward(value_buf, value_send, value_recv)

    scale = 1.0 / math.sqrt(HEAD_DIM)
    across = (((1,), (1,)), ((), ()))
    held = []
    for head in range(heads):
        lanes = slice(head * HEAD_DIM, (head + 1) * HEAD_DIM)
        turned = query_rot[:, lanes]
        short = key_buf[:, :, lanes].reshape(places * patches, HEAD_DIM)
        text = text_all[0, :, lanes].astype(jnp.bfloat16)
        short_scores = lax.dot_general(turned, short, across, preferred_element_type=jnp.float32)
        text_scores = lax.dot_general(turned, text, across, preferred_element_type=jnp.float32)
        top = jnp.maximum(
            jnp.max(short_scores, axis=-1, keepdims=True), jnp.max(text_scores, axis=-1, keepdims=True)
        )
        short_weights = jnp.exp((short_scores - top) * scale).astype(jnp.bfloat16)
        text_weights = jnp.exp((text_scores - top) * scale).astype(jnp.bfloat16)
        total = jnp.sum(short_weights.astype(jnp.float32), axis=-1, keepdims=True) + jnp.sum(
            text_weights.astype(jnp.float32), axis=-1, keepdims=True
        )
        held.append((short_weights, text_weights, 1.0 / total))

    collect(value_buf, value_send, value_recv)
    for head in range(heads):
        lanes = slice(head * HEAD_DIM, (head + 1) * HEAD_DIM)
        short_weights, text_weights, inverse = held[head]
        short = value_buf[:, :, lanes].reshape(places * patches, HEAD_DIM)
        text = text_all[1, :, lanes].astype(jnp.bfloat16)
        summed = jnp.dot(short_weights, short, preferred_element_type=jnp.float32) + jnp.dot(
            text_weights, text, preferred_element_type=jnp.float32
        )
        attended[:, lanes] = (summed * inverse).astype(jnp.bfloat16)

    loads[5].wait()
    exchanges = []
    for part in range(parts):
        lanes = slice(part * part_width, (part + 1) * part_width)
        own_part[part] = jnp.dot(
            attended[...], weight_buf[:, lanes], preferred_element_type=jnp.float32
        ).astype(jnp.bfloat16)
        exchange = pltpu.make_async_remote_copy(
            src_ref=own_part.at[part],
            dst_ref=peer_part.at[part],
            send_sem=part_send.at[part],
            recv_sem=part_recv.at[part],
            device_id={"tensor": 1 - core},
            device_id_type=MESH,
        )
        exchange.start()
        exchanges.append(exchange)
    loads[6].wait()
    for part in range(parts):
        lanes = slice(part * part_width, (part + 1) * part_width)
        exchanges[part].wait_recv()
        projected = own_part[part].astype(jnp.float32) + peer_part[part].astype(jnp.float32)
        mixed[:, lanes] = (
            hidden_buf[:, lanes].astype(jnp.float32) + gate[:, lanes].astype(jnp.float32) * projected
        ).astype(jnp.bfloat16)
    for copy in sends + exchanges:
        copy.wait_send()


def local(
    places, queries, keys, values, text_keys, text_values, conv_weight, out_weight, image_hidden, gate
):
    tokens, features = queries.shape
    width = out_weight.shape[1]
    patches = tokens // 4
    text_rows = text_keys.shape[0]
    inner = 1 << ((places.bit_length() - 1) // 2)
    if places % inner:
        inner = 1
    row_table, col_table = position_tables(places, tokens // 2)
    parts = 3
    bf16, f32 = jnp.bfloat16, jnp.float32
    hbm = pl.BlockSpec(memory_space=pl.ANY)
    vmem = pl.BlockSpec(memory_space=pltpu.VMEM)
    sems = pltpu.SemaphoreType.DMA
    return pl.pallas_call(
        functools.partial(fused, places, inner),
        out_shape=jax.ShapeDtypeStruct((tokens, width), bf16),
        in_specs=[hbm, hbm, hbm, hbm, hbm, vmem, hbm, hbm, vmem, vmem, vmem],
        out_specs=vmem,
        scratch_shapes=[
            pltpu.VMEM((places, patches, features), bf16),
            pltpu.VMEM((places, patches, features), bf16),
            pltpu.VMEM((places, 2, text_rows, features), bf16),
            pltpu.VMEM((2, places * text_rows, features), f32),
            pltpu.VMEM((tokens, features), bf16),
            pltpu.VMEM((tokens, features), bf16),
            pltpu.VMEM((tokens, features), bf16),
            pltpu.VMEM((features, width), bf16),
            pltpu.VMEM((tokens, width), bf16),
            pltpu.VMEM((tokens, features), bf16),
            pltpu.VMEM((tokens, features), bf16),
            pltpu.VMEM((parts, tokens, width // parts), bf16),
            pltpu.VMEM((parts, tokens, width // parts), bf16),
            sems((7,)),
            sems((places,)),
            sems((places,)),
            sems((places,)),
            sems((places,)),
            sems((places,)),
            sems((places,)),
            sems((parts,)),
            sems((parts,)),
        ],
        compiler_params=pltpu.CompilerParams(collective_id=0, has_side_effects=True),
        name="joint_attention",
    )(
        queries, keys, values, text_keys, text_values, conv_weight, out_weight, image_hidden,
        gate.reshape(1, width), jnp.asarray(row_table), jnp.asarray(col_table),
    )


def solution(mesh):
    placed = (
        P(("groups", "seq"), "tensor"),
        P(("groups", "seq"), "tensor"),
        P(("groups", "seq"), "tensor"),
        P(("groups", "seq"), "tensor"),
        P(("groups", "seq"), "tensor"),
        P(None, "tensor"),
        P("tensor", None),
        P(("groups", "seq"), None),
        P("groups"),
    )
    return jax.shard_map(
        functools.partial(local, mesh.shape["seq"]),
        mesh=mesh,
        in_specs=placed,
        out_specs=P(("groups", "seq"), None),
        check_vma=False,
    )
```

time: 192 us -> 28.2 us (0.15)
  blocking collectives: 125 us -> 0 us
  Pallas kernels: 0 us -> 24.6 us
  waiting for transfers between devices: 19.4 us -> 0 us
  between operations: 13.6 us -> 0.01 us
  other arithmetic: 13.3 us -> 0 us
  local copies, waits for them, and re-layouts: 12.9 us -> 3.05 us
  matrix products: 7.08 us -> 0 us
    all_gather x4 -> x0, blocking collectives: 125 us -> none  [the longest x1 32.8 us: local(): lax.all_gather(short_keys, 'seq', axis=0, tiled=True)]
    pallas_call x0 -> x1, Pallas kernels: none -> 24.6 us  [local(): pl.pallas_call(functools.partial(fused, places, inner), out_shape=jax.Sha...]
    psum x1 -> x0, waiting for transfers between devices: 19.4 us -> none  [local(): lax.psum(jnp.dot(attended, out_weight, preferred_element_type=jnp.float32...]
    dot_general x5 -> x0, matrix products: 7.08 us -> none  [the longest x2 3.46 us: absorb_block(): jnp.einsum('hqk,khd->qhd', weights, value_heads, preferred_element_type=j...]
    add x4 -> x0, other arithmetic: 4.69 us -> none  [the longest x1 3.4 us: compress(): grid_cells[0, :, 0] * tap_grid[0, 0] + grid_cells[0, :, 1] * tap_grid[0, 1]]
    mul x4 -> x0, local copies, waits for them, and re-layouts: 3.36 us -> none  [the longest x1 0.85 us: compress(): grid_cells[1, :, 0] * tap_grid[1, 0]]
    another operation x6 -> x0, other arithmetic: 2.86 us -> none
    convert_element_type x4 -> x0, other arithmetic: 2.48 us -> none  [the longest x1 1.86 us: local(): return (image_hidden.astype(jnp.float32) + gate.astype(jnp.float32)[None,...]
  transfers between devices with their start and end apart: 1 -> 0, of which waited for: 1 -> 0; matrix products, arithmetic and copies ran while one was open for 0% -> 0% of each run, Pallas kernels for 0% -> 0%
where the time goes in v1:
time: 28.2 us; the launch traced here: 27.7 us
  Pallas kernels  24.6 us (87%)
  local copies, waits for them, and re-layouts  3.05 us (11%)
    pallas_call x1, Pallas kernels, local(): pl.pallas_call(functools.partial(fused, places, inner), out_shape=jax.Sha...  24.6 us
    unnamed x1, local copies, waits for them, and re-layouts  1.77 us
    reshape x1, local copies, waits for them, and re-layouts, local(): gate.reshape(1, width)  1.28 us

profile of v1, /device:TPU:0, one launch (start us, length us, event | category | flops | bytes accessed | tf_op | source)
XLA Modules:
  0.0 27.7 jit_solution(12663819241735986234)
XLA Ops:
  0.0 1.3 %reshape.3.gate = bf16[1,1536]{1,0:T(2,128)(2,1)} reshape(bf16[1536]{0:T(1024)(128)(2,1)} %param.19) | data formatting | bytes 6144 | tf_op jit(solution)/shard_map/reshape | solution.py:323
  1.3 24.6 %joint_attention.1 = bf16[128,1536]{1,0:T(8,128)(2,1)} custom-call(bf16[128,768]{1,0:T(8,128)(2,1)} %queries.1, bf16[128,768]{1,0:T(8,128)(2,1)} %keys.1, bf16[128,768]{1,0:T(8,128)(2,1)} %values.1, bf16[4,768]{1,0:T(4,128)(2,1)} %text_keys.1, bf16[4,768]{1,0:T(4,128)(2,1)} %text_values.1, bf16[4,768]{1,0:T(4,128)(2,1)} %conv_weight.1, ...), custom_call_target="tpu_custom_call" | custom-call | tf_op jit(solution)/shard_map/joint_attention/pallas_call | solution.py:290
  25.9 1.8 %copy.13 = bf16[128,1536]{1,0:T(8,128)(2,1)} copy(bf16[128,1536]{1,0:T(8,128)(2,1)} %joint_attention.1) | data formatting | bytes 786432

commit v2 on v1

v2 whole, which is shorter than its diff:
```python
import functools
import math

import jax
import jax.numpy as jnp
import numpy as np
from jax import lax
from jax.experimental import pallas as pl
from jax.experimental.pallas import tpu as pltpu
from jax.sharding import PartitionSpec as P

HEAD_DIM = 128
MESH = pl.DeviceIdType.MESH


def position_tables(places, row_width):
    lead = HEAD_DIM // 8
    group = HEAD_DIM * 7 // 16
    frequency = np.power(
        np.float32(10000.0), -(2.0 * np.arange(group // 2, dtype=np.float32)) / np.float32(group)
    ).astype(np.float32)
    pair_frequency = np.repeat(frequency, 2)
    sign = np.where(np.arange(group) % 2 == 0, -1.0, 1.0)

    def turned(positions):
        angles = (np.asarray(positions, np.float32)[:, None] * pair_frequency[None, :]).astype(np.float64)
        return np.cos(angles), np.sin(angles) * sign

    def row_part(positions):
        cos_part, sin_part = turned(positions)
        count = len(positions)
        full_cos = np.zeros((count, HEAD_DIM))
        full_sin = np.zeros((count, HEAD_DIM))
        full_cos[:, :lead] = 1.0
        full_cos[:, lead : lead + group] = cos_part
        full_sin[:, lead : lead + group] = sin_part
        return full_cos, full_sin

    def col_part(positions):
        cos_part, sin_part = turned(positions)
        count = len(positions)
        full_cos = np.zeros((count, HEAD_DIM))
        full_sin = np.zeros((count, HEAD_DIM))
        full_cos[:, lead + group :] = cos_part
        full_sin[:, lead + group :] = sin_part
        return full_cos, full_sin

    place = np.arange(places, dtype=np.float32)
    rows = np.zeros((places, 8, HEAD_DIM))
    rows[:, 0], rows[:, 2] = row_part(2.0 * place)
    rows[:, 1], rows[:, 3] = row_part(2.0 * place + 1.0)
    rows[:, 4], rows[:, 5] = row_part(2.0 * place + 0.5)
    cos_q, sin_q = col_part(np.arange(row_width))
    cos_k, sin_k = col_part(2.0 * np.arange(row_width // 2) + 0.5)
    cols = np.concatenate([cos_q, sin_q, cos_k, sin_k], axis=0)
    return rows.astype(np.float32), cols.astype(np.float32)


def fused(
    places, inner, queries, keys, values, text_keys, text_values, conv_weight, out_weight, image_hidden,
    gate, row_table, col_table, mixed, key_buf, value_buf, text_buf, text_all, query_in, key_in, value_in,
    weight_buf, hidden_buf, taps_buf, gate_buf, rows_buf, cols_buf, query_rot, attended, own_part, peer_part,
    load_sem, key_send, key_recv, value_send, value_recv, text_send, text_recv, part_send, part_recv,
):
    tokens, features = query_in.shape
    heads = features // HEAD_DIM
    row_width = tokens // 2
    patches = row_width // 2
    text_rows = text_keys.shape[0]
    outer = places // inner
    parts = own_part.shape[0]
    part_width = own_part.shape[2]
    me = lax.axis_index("seq")
    core = lax.axis_index("tensor")
    along = me // inner
    across = lax.rem(me, inner)
    inner_peers = [lax.rem(across + step, inner) for step in range(1, inner)]

    def at_place(outer_at, inner_at):
        return {"seq": outer_at * inner + inner_at}

    def inside(outer_at):
        return jnp.logical_and(outer_at >= 0, outer_at < outer)

    barrier = pltpu.get_barrier_semaphore()
    near = [move for move in (1, -1, 2, -2) if abs(move) < outer]
    for move in near:

        @pl.when(inside(along + move))
        def _():
            pl.semaphore_signal(
                barrier, inc=1, device_id=at_place(along + move, across), device_id_type=MESH
            )

    for peer in inner_peers:
        pl.semaphore_signal(barrier, inc=1, device_id=at_place(along, peer), device_id_type=MESH)
    pl.semaphore_signal(barrier, inc=1, device_id={"tensor": 1 - core}, device_id_type=MESH)

    loads = [
        pltpu.make_async_copy(keys, key_in, load_sem.at[0]),
        pltpu.make_async_copy(conv_weight, taps_buf, load_sem.at[1]),
        pltpu.make_async_copy(row_table.at[me], rows_buf, load_sem.at[2]),
        pltpu.make_async_copy(col_table, cols_buf, load_sem.at[3]),
        pltpu.make_async_copy(values, value_in, load_sem.at[4]),
        pltpu.make_async_copy(text_keys, text_buf.at[across, along, 0], load_sem.at[5]),
        pltpu.make_async_copy(text_values, text_buf.at[across, along, 1], load_sem.at[6]),
        pltpu.make_async_copy(queries, query_in, load_sem.at[7]),
        pltpu.make_async_copy(out_weight, weight_buf, load_sem.at[8]),
        pltpu.make_async_copy(image_hidden, hidden_buf, load_sem.at[9]),
        pltpu.make_async_copy(gate, gate_buf, load_sem.at[10]),
    ]
    for load in loads:
        load.start()

    row_of = lax.broadcasted_iota(jnp.int32, (tokens, tokens), 0)
    token_of = lax.broadcasted_iota(jnp.int32, (tokens, tokens), 1)
    tap_of = row_of // patches
    wanted = (tap_of // 2) * row_width + 2 * (row_of % patches) + tap_of % 2
    pick = (token_of == wanted).astype(jnp.bfloat16)
    for load in loads[:4]:
        load.wait()
    taps = taps_buf[...].astype(jnp.float32)

    def compress(field):
        picked = jnp.dot(pick, field, preferred_element_type=jnp.float32)
        total = picked[:patches] * taps[0:1]
        for tap in range(1, 4):
            total = total + picked[tap * patches : (tap + 1) * patches] * taps[tap : tap + 1]
        return total

    my_rows = rows_buf[...]
    cos_k = my_rows[4:5] + cols_buf[2 * row_width : 2 * row_width + patches]
    sin_k = my_rows[5:6] + cols_buf[2 * row_width + patches : 2 * row_width + 2 * patches]
    even = lax.broadcasted_iota(jnp.int32, (patches, HEAD_DIM), 1) % 2 == 0
    short_raw = compress(key_in[...])
    for head in range(heads):
        lanes = slice(head * HEAD_DIM, (head + 1) * HEAD_DIM)
        raw = short_raw[:, lanes]
        swapped = jnp.where(even, pltpu.roll(raw, HEAD_DIM - 1, 1), pltpu.roll(raw, 1, 1))
        key_buf[across, along, :, lanes] = (raw * cos_k + swapped * sin_k).astype(jnp.bfloat16)
    loads[4].wait()
    value_buf[across, along] = compress(value_in[...]).astype(jnp.bfloat16)
    loads[5].wait()
    loads[6].wait()

    pl.semaphore_wait(barrier, inner + sum(inside(along + move).astype(jnp.int32) for move in near))

    closing = []

    def copy_of(buf, slot, send_sem, recv_sem, number, target):
        return pltpu.make_async_remote_copy(
            src_ref=buf.at[slot[0], slot[1]],
            dst_ref=buf.at[slot[0], slot[1]],
            send_sem=send_sem.at[number],
            recv_sem=recv_sem.at[slot[0], slot[1]],
            device_id=target,
            device_id_type=MESH,
        )

    def send(buf, slot, send_sem, recv_sem, number, target, when=None):
        def begin():
            copy_of(buf, slot, send_sem, recv_sem, number, target).start()

        def end():
            copy_of(buf, slot, send_sem, recv_sem, number, target).wait_send()

        if when is None:
            begin()
            closing.append(end)
        else:
            pl.when(when)(begin)
            closing.append(lambda: pl.when(when)(end))

    def send_own(buf, send_sem, recv_sem):
        for number, move in enumerate(near):
            send(
                buf, (across, along), send_sem, recv_sem, number, at_place(along + move, across),
                inside(along + move),
            )
        for number, peer in enumerate(inner_peers):
            send(buf, (across, along), send_sem, recv_sem, 4 + number, at_place(along, peer))

    def pass_on(buf, send_sem, recv_sem):
        number = 4 + inner - 1
        for distance in range(1, outer):
            for side in (1, -1):
                source = along + side * distance
                slot = (across, jnp.clip(source, 0, outer - 1))
                here = inside(source)

                @pl.when(here)
                def _():
                    copy_of(buf, slot, send_sem, recv_sem, 0, at_place(along, across)).wait_recv()

                further = along - 2 * side
                send(
                    buf, slot, send_sem, recv_sem, number, at_place(further, across),
                    jnp.logical_and(here, inside(further)),
                )
                number += 1
                for peer in inner_peers:
                    send(buf, slot, send_sem, recv_sem, number, at_place(along, peer), here)
                    number += 1

    def collect(buf, send_sem, recv_sem):
        for peer in inner_peers:
            for place in range(outer):
                copy_of(buf, (peer, place), send_sem, recv_sem, 0, at_place(along, across)).wait_recv()

    send_own(key_buf, key_send, key_recv)
    send_own(text_buf, text_send, text_recv)
    send_own(value_buf, value_send, value_recv)

    loads[7].wait()
    first = lax.broadcasted_iota(jnp.int32, (HEAD_DIM, HEAD_DIM), 0)
    second = lax.broadcasted_iota(jnp.int32, (HEAD_DIM, HEAD_DIM), 1)
    swap = (first == second + 1 - 2 * (second % 2)).astype(jnp.bfloat16)
    col_cos = cols_buf[:row_width]
    col_sin = cols_buf[row_width : 2 * row_width]
    for row in range(2):
        cos_q = my_rows[row : row + 1] + col_cos
        sin_q = my_rows[2 + row : 3 + row] + col_sin
        rows = slice(row * row_width, (row + 1) * row_width)
        for head in range(heads):
            lanes = slice(head * HEAD_DIM, (head + 1) * HEAD_DIM)
            plain = query_in[rows, lanes]
            crossed = jnp.dot(plain, swap, preferred_element_type=jnp.float32)
            query_rot[rows, lanes] = (plain.astype(jnp.float32) * cos_q + crossed * sin_q).astype(jnp.bfloat16)

    pass_on(key_buf, key_send, key_recv)
    pass_on(text_buf, text_send, text_recv)
    pass_on(value_buf, value_send, value_recv)

    scale = 1.0 / math.sqrt(HEAD_DIM)
    transposed = (((1,), (1,)), ((), ()))
    lanes_of = [slice(head * HEAD_DIM, (head + 1) * HEAD_DIM) for head in range(heads)]

    def scores_with(keys_of):
        return [
            lax.dot_general(query_rot[:, lanes], keys_of(lanes), transposed, preferred_element_type=jnp.float32)
            for lanes in lanes_of
        ]

    def group_of(buf, at):
        return lambda lanes: buf[at, :, :, lanes].reshape(outer * patches, HEAD_DIM)

    scores = [scores_with(group_of(key_buf, across))]
    collect(text_buf, text_send, text_recv)
    for kind in range(2):
        for place in range(places):
            text_all[kind, place * text_rows : (place + 1) * text_rows, :] = text_buf[
                place // outer, place % outer, kind
            ].astype(jnp.float32)
    scores.append(scores_with(lambda lanes: text_all[0, :, lanes].astype(jnp.bfloat16)))
    collect(key_buf, key_send, key_recv)
    for peer in inner_peers:
        scores.append(scores_with(group_of(key_buf, peer)))

    weights, inverse = [], []
    for head in range(heads):
        top = functools.reduce(
            jnp.maximum, [jnp.max(group[head], axis=-1, keepdims=True) for group in scores]
        )
        weights.append([jnp.exp((group[head] - top) * scale).astype(jnp.bfloat16) for group in scores])
        total = sum(jnp.sum(group.astype(jnp.float32), axis=-1, keepdims=True) for group in weights[head])
        inverse.append(1.0 / total)
    summed = [
        jnp.dot(weights[head][0], group_of(value_buf, across)(lanes), preferred_element_type=jnp.float32)
        + jnp.dot(
            weights[head][1], text_all[1, :, lanes].astype(jnp.bfloat16), preferred_element_type=jnp.float32
        )
        for head, lanes in enumerate(lanes_of)
    ]
    loads[8].wait()
    loads[9].wait()
    loads[10].wait()

    collect(value_buf, value_send, value_recv)
    for head, lanes in enumerate(lanes_of):
        for number, peer in enumerate(inner_peers):
            summed[head] = summed[head] + jnp.dot(
                weights[head][2 + number], group_of(value_buf, peer)(lanes), preferred_element_type=jnp.float32
            )
        attended[:, lanes] = (summed[head] * inverse[head]).astype(jnp.bfloat16)

    exchanges = []
    for part in range(parts):
        lanes = slice(part * part_width, (part + 1) * part_width)
        own_part[part] = jnp.dot(
            attended[...], weight_buf[:, lanes], preferred_element_type=jnp.float32
        ).astype(jnp.bfloat16)
        exchange = pltpu.make_async_remote_copy(
            src_ref=own_part.at[part],
            dst_ref=peer_part.at[part],
            send_sem=part_send.at[part],
            recv_sem=part_recv.at[part],
            device_id={"tensor": 1 - core},
            device_id_type=MESH,
        )
        exchange.start()
        exchanges.append(exchange)
    for end in closing:
        end()
    gates = gate_buf[...].astype(jnp.float32).reshape(1, parts * part_width)
    for part in range(parts):
        lanes = slice(part * part_width, (part + 1) * part_width)
        exchanges[part].wait_recv()
        projected = own_part[part].astype(jnp.float32) + peer_part[part].astype(jnp.float32)
        mixed[:, lanes] = (
            hidden_buf[:, lanes].astype(jnp.float32) + gates[:, lanes] * projected
        ).astype(jnp.bfloat16)
    for exchange in exchanges:
        exchange.wait_send()


def local(
    places, queries, keys, values, text_keys, text_values, conv_weight, out_weight, image_hidden, gate
):
    tokens, features = queries.shape
    width = out_weight.shape[1]
    patches = tokens // 4
    text_rows = text_keys.shape[0]
    inner = 1 << ((places.bit_length() - 1) // 2)
    if places % inner:
        inner = 1
    row_table, col_table = position_tables(places, tokens // 2)
    parts = 3
    bf16, f32 = jnp.bfloat16, jnp.float32
    hbm = pl.BlockSpec(memory_space=pl.ANY)
    vmem = pl.BlockSpec(memory_space=pltpu.VMEM)
    sems = pltpu.SemaphoreType.DMA
    outer = places // inner
    sends = 4 + inner - 1 + 2 * (outer - 1) * inner
    return pl.pallas_call(
        functools.partial(fused, places, inner),
        out_shape=pltpu.VMEM((tokens, width), bf16),
        in_specs=[hbm] * 11,
        out_specs=vmem,
        scratch_shapes=[
            pltpu.VMEM((inner, outer, patches, features), bf16),
            pltpu.VMEM((inner, outer, patches, features), bf16),
            pltpu.VMEM((inner, outer, 2, text_rows, features), bf16),
            pltpu.VMEM((2, places * text_rows, features), f32),
            pltpu.VMEM((tokens, features), bf16),
            pltpu.VMEM((tokens, features), bf16),
            pltpu.VMEM((tokens, features), bf16),
            pltpu.VMEM((features, width), bf16),
            pltpu.VMEM((tokens, width), bf16),
            pltpu.VMEM(conv_weight.shape, bf16),
            pltpu.VMEM(gate.shape, bf16),
            pltpu.VMEM(row_table.shape[1:], f32),
            pltpu.VMEM(col_table.shape, f32),
            pltpu.VMEM((tokens, features), bf16),
            pltpu.VMEM((tokens, features), bf16),
            pltpu.VMEM((parts, tokens, width // parts), bf16),
            pltpu.VMEM((parts, tokens, width // parts), bf16),
            sems((11,)),
            sems((sends,)),
            sems((inner, outer)),
            sems((sends,)),
            sems((inner, outer)),
            sems((sends,)),
            sems((inner, outer)),
            sems((parts,)),
            sems((parts,)),
        ],
        compiler_params=pltpu.CompilerParams(collective_id=0, has_side_effects=True),
        name="joint_attention",
    )(
        queries, keys, values, text_keys, text_values, conv_weight, out_weight, image_hidden,
        gate, jnp.asarray(row_table), jnp.asarray(col_table),
    )


def solution(mesh):
    placed = (
        P(("groups", "seq"), "tensor"),
        P(("groups", "seq"), "tensor"),
        P(("groups", "seq"), "tensor"),
        P(("groups", "seq"), "tensor"),
        P(("groups", "seq"), "tensor"),
        P(None, "tensor"),
        P("tensor", None),
        P(("groups", "seq"), None),
        P("groups"),
    )
    return jax.shard_map(
        functools.partial(local, mesh.shape["seq"]),
        mesh=mesh,
        in_specs=placed,
        out_specs=P(("groups", "seq"), None),
        check_vma=False,
    )
```

time: 28.2 us -> 24.7 us (0.88); the launches traced: 27.7 us -> 24.5 us
  local copies, waits for them, and re-layouts: 3.05 us -> 0.75 us
  Pallas kernels: 24.6 us -> 23.8 us
    reshape x1 -> x0, local copies, waits for them, and re-layouts: 1.28 us -> none  [local(): gate.reshape(1, width)]
    unnamed x1, local copies, waits for them, and re-layouts: 1.77 us -> 0.75 us
    pallas_call x1, Pallas kernels: 24.6 us -> 23.8 us  [local(): pl.pallas_call(functools.partial(fused, places, inner), out_shape=pltpu.V...]
where the time goes in v2:
time: 24.7 us; the launch traced here: 24.5 us
  Pallas kernels  23.8 us (96%)
  local copies, waits for them, and re-layouts  0.75 us (3%)
    pallas_call x1, Pallas kernels, local(): pl.pallas_call(functools.partial(fused, places, inner), out_shape=pltpu.V...  23.8 us
    unnamed x1, local copies, waits for them, and re-layouts  0.75 us

profile of v2, /device:TPU:0, one launch (start us, length us, event | category | flops | bytes accessed | tf_op | source)
XLA Modules:
  0.0 24.5 jit_solution(7339242121946266373)
XLA Ops:
  0.0 23.8 %joint_attention.1 = bf16[128,1536]{1,0:T(8,128)(2,1)S(1)} custom-call(bf16[128,768]{1,0:T(8,128)(2,1)} %queries.1, bf16[128,768]{1,0:T(8,128)(2,1)} %keys.1, bf16[128,768]{1,0:T(8,128)(2,1)} %values.1, bf16[4,768]{1,0:T(4,128)(2,1)} %text_keys.1, bf16[4,768]{1,0:T(4,128)(2,1)} %text_values.1, bf16[4,768]{1,0:T(4,128)(2,1)} %conv_weight.1, ...), custom_call_target="tpu_custom_call" | custom-call | tf_op jit(solution)/shard_map/joint_attention/pallas_call | solution.py:334
  23.8 0.7 %copy.13 = bf16[128,1536]{1,0:T(8,128)(2,1)} copy(bf16[128,1536]{1,0:T(8,128)(2,1)S(1)} %joint_attention.1) | data formatting | bytes 786432

commit v3 on v2

--- a/solution.py
+++ b/solution.py
@@ -10,6 +10,7 @@
 from jax.sharding import PartitionSpec as P
 
 HEAD_DIM = 128
+REACH = 1
 MESH = pl.DeviceIdType.MESH
 
 
@@ -58,9 +59,9 @@
 
 def fused(
     places, inner, queries, keys, values, text_keys, text_values, conv_weight, out_weight, image_hidden,
-    gate, row_table, col_table, mixed, key_buf, value_buf, text_buf, text_all, query_in, key_in, value_in,
+    gate, row_table, col_table, mixed, key_buf, value_buf, text_in, text_all, query_in, key_in, value_in,
     weight_buf, hidden_buf, taps_buf, gate_buf, rows_buf, cols_buf, query_rot, attended, own_part, peer_part,
-    load_sem, key_send, key_recv, value_send, value_recv, text_send, text_recv, part_send, part_recv,
+    load_sem, key_send, key_recv, value_send, value_recv, part_send, part_recv,
 ):
     tokens, features = query_in.shape
     heads = features // HEAD_DIM
@@ -83,7 +84,7 @@
         return jnp.logical_and(outer_at >= 0, outer_at < outer)
 
     barrier = pltpu.get_barrier_semaphore()
-    near = [move for move in (1, -1, 2, -2) if abs(move) < outer]
+    near = [side * step for step in range(1, min(REACH, outer - 1) + 1) for side in (1, -1)]
     for move in near:
 
         @pl.when(inside(along + move))
@@ -102,8 +103,8 @@
         pltpu.make_async_copy(row_table.at[me], rows_buf, load_sem.at[2]),
         pltpu.make_async_copy(col_table, cols_buf, load_sem.at[3]),
         pltpu.make_async_copy(values, value_in, load_sem.at[4]),
-        pltpu.make_async_copy(text_keys, text_buf.at[across, along, 0], load_sem.at[5]),
-        pltpu.make_async_copy(text_values, text_buf.at[across, along, 1], load_sem.at[6]),
+        pltpu.make_async_copy(text_keys, text_in.at[0], load_sem.at[5]),
+        pltpu.make_async_copy(text_values, text_in.at[1], load_sem.at[6]),
         pltpu.make_async_copy(queries, query_in, load_sem.at[7]),
         pltpu.make_async_copy(out_weight, weight_buf, load_sem.at[8]),
         pltpu.make_async_copy(image_hidden, hidden_buf, load_sem.at[9]),
@@ -137,17 +138,21 @@
         lanes = slice(head * HEAD_DIM, (head + 1) * HEAD_DIM)
         raw = short_raw[:, lanes]
         swapped = jnp.where(even, pltpu.roll(raw, HEAD_DIM - 1, 1), pltpu.roll(raw, 1, 1))
-        key_buf[across, along, :, lanes] = (raw * cos_k + swapped * sin_k).astype(jnp.bfloat16)
+        key_buf[across, along, :patches, lanes] = (raw * cos_k + swapped * sin_k).astype(jnp.bfloat16)
     loads[4].wait()
     value_buf[across, along] = compress(value_in[...]).astype(jnp.bfloat16)
     loads[5].wait()
     loads[6].wait()
+    key_buf[across, along, patches:, :] = jnp.concatenate(
+        [text_in[kind].astype(jnp.float32) for kind in range(2)], axis=0
+    ).astype(jnp.bfloat16)
 
     pl.semaphore_wait(barrier, inner + sum(inside(along + move).astype(jnp.int32) for move in near))
 
     closing = []
 
-    def copy_of(buf, slot, send_sem, recv_sem, number, target):
+    def copy_of(kind, slot, number, target):
+        buf, send_sem, recv_sem = kind
         return pltpu.make_async_remote_copy(
             src_ref=buf.at[slot[0], slot[1]],
             dst_ref=buf.at[slot[0], slot[1]],
@@ -157,12 +162,12 @@
             device_id_type=MESH,
         )
 
-    def send(buf, slot, send_sem, recv_sem, number, target, when=None):
+    def send(kind, slot, number, target, when=None):
         def begin():
-            copy_of(buf, slot, send_sem, recv_sem, number, target).start()
+            copy_of(kind, slot, number, target).start()
 
         def end():
-            copy_of(buf, slot, send_sem, recv_sem, number, target).wait_send()
+            copy_of(kind, slot, number, target).wait_send()
 
         if when is None:
             begin()
@@ -171,45 +176,42 @@
             pl.when(when)(begin)
             closing.append(lambda: pl.when(when)(end))
 
-    def send_own(buf, send_sem, recv_sem):
-        for number, move in enumerate(near):
-            send(
-                buf, (across, along), send_sem, recv_sem, number, at_place(along + move, across),
-                inside(along + move),
-            )
-        for number, peer in enumerate(inner_peers):
-            send(buf, (across, along), send_sem, recv_sem, 4 + number, at_place(along, peer))
-
-    def pass_on(buf, send_sem, recv_sem):
-        number = 4 + inner - 1
+    def await_arrival(kind, slot):
+        copy_of(kind, slot, 0, at_place(along, across)).wait_recv()
+
+    carried = ((key_buf, key_send, key_recv), (value_buf, value_send, value_recv))
+
+    def send_own():
+        for kind in carried:
+            for number, move in enumerate(near):
+                send(kind, (across, along), number, at_place(along + move, across), inside(along + move))
+            for number, peer in enumerate(inner_peers):
+                send(kind, (across, along), len(near) + number, at_place(along, peer))
+
+    def pass_on():
+        first_number = len(near) + inner - 1
         for distance in range(1, outer):
-            for side in (1, -1):
-                source = along + side * distance
-                slot = (across, jnp.clip(source, 0, outer - 1))
-                here = inside(source)
-
-                @pl.when(here)
-                def _():
-                    copy_of(buf, slot, send_sem, recv_sem, 0, at_place(along, across)).wait_recv()
-
-                further = along - 2 * side
-                send(
-                    buf, slot, send_sem, recv_sem, number, at_place(further, across),
-                    jnp.logical_and(here, inside(further)),
-                )
-                number += 1
-                for peer in inner_peers:
-                    send(buf, slot, send_sem, recv_sem, number, at_place(along, peer), here)
+            for at, kind in enumerate(carried):
+                number = first_number + 2 * (distance - 1) * inner
+                for side in (1, -1):
+                    source = along + side * distance
+                    slot = (across, jnp.clip(source, 0, outer - 1))
+                    here = inside(source)
+                    pl.when(here)(functools.partial(await_arrival, kind, slot))
+                    if distance >= REACH:
+                        further = along - side
+                        send(kind, slot, number, at_place(further, across), jnp.logical_and(here, inside(further)))
                     number += 1
-
-    def collect(buf, send_sem, recv_sem):
+                    for peer in inner_peers:
+                        send(kind, slot, number, at_place(along, peer), here)
+                        number += 1
+
+    def collect(kind):
         for peer in inner_peers:
             for place in range(outer):
-                copy_of(buf, (peer, place), send_sem, recv_sem, 0, at_place(along, across)).wait_recv()
-
-    send_own(key_buf, key_send, key_recv)
-    send_own(text_buf, text_send, text_recv)
-    send_own(value_buf, value_send, value_recv)
+                await_arrival(kind, (peer, place))
+
+    send_own()
 
     loads[7].wait()
     first = lax.broadcasted_iota(jnp.int32, (HEAD_DIM, HEAD_DIM), 0)
@@ -227,9 +229,7 @@
             crossed = jnp.dot(plain, swap, preferred_element_type=jnp.float32)
             query_rot[rows, lanes] = (plain.astype(jnp.float32) * cos_q + crossed * sin_q).astype(jnp.bfloat16)
 
-    pass_on(key_buf, key_send, key_recv)
-    pass_on(text_buf, text_send, text_recv)
-    pass_on(value_buf, value_send, value_recv)
+    pass_on()
 
     scale = 1.0 / math.sqrt(HEAD_DIM)
     transposed = (((1,), (1,)), ((), ()))
@@ -242,17 +242,17 @@
         ]
 
     def group_of(buf, at):
-        return lambda lanes: buf[at, :, :, lanes].reshape(outer * patches, HEAD_DIM)
+        return lambda lanes: buf[at, :, :patches, lanes].reshape(outer * patches, HEAD_DIM)
 
     scores = [scores_with(group_of(key_buf, across))]
-    collect(text_buf, text_send, text_recv)
+    collect(carried[0])
     for kind in range(2):
         for place in range(places):
-            text_all[kind, place * text_rows : (place + 1) * text_rows, :] = text_buf[
-                place // outer, place % outer, kind
+            start = patches + kind * text_rows
+            text_all[kind, place * text_rows : (place + 1) * text_rows, :] = key_buf[
+                place // outer, place % outer, start : start + text_rows
             ].astype(jnp.float32)
     scores.append(scores_with(lambda lanes: text_all[0, :, lanes].astype(jnp.bfloat16)))
-    collect(key_buf, key_send, key_recv)
     for peer in inner_peers:
         scores.append(scores_with(group_of(key_buf, peer)))
 
@@ -275,7 +275,7 @@
     loads[9].wait()
     loads[10].wait()
 
-    collect(value_buf, value_send, value_recv)
+    collect(carried[1])
     for head, lanes in enumerate(lanes_of):
         for number, peer in enumerate(inner_peers):
             summed[head] = summed[head] + jnp.dot(
@@ -330,16 +330,16 @@
     vmem = pl.BlockSpec(memory_space=pltpu.VMEM)
     sems = pltpu.SemaphoreType.DMA
     outer = places // inner
-    sends = 4 + inner - 1 + 2 * (outer - 1) * inner
+    sends = 2 * REACH + inner - 1 + 2 * (outer - 1) * inner
     return pl.pallas_call(
         functools.partial(fused, places, inner),
         out_shape=pltpu.VMEM((tokens, width), bf16),
         in_specs=[hbm] * 11,
         out_specs=vmem,
         scratch_shapes=[
+            pltpu.VMEM((inner, outer, patches + 2 * text_rows, features), bf16),
             pltpu.VMEM((inner, outer, patches, features), bf16),
-            pltpu.VMEM((inner, outer, patches, features), bf16),
-            pltpu.VMEM((inner, outer, 2, text_rows, features), bf16),
+            pltpu.VMEM((2, text_rows, features), bf16),
             pltpu.VMEM((2, places * text_rows, features), f32),
             pltpu.VMEM((tokens, features), bf16),
             pltpu.VMEM((tokens, features), bf16),
@@ -355,8 +355,6 @@
             pltpu.VMEM((parts, tokens, width // parts), bf16),
             pltpu.VMEM((parts, tokens, width // parts), bf16),
             sems((11,)),
-            sems((sends,)),
-            sems((inner, outer)),
             sems((sends,)),
             sems((inner, outer)),
             sems((sends,)),

time: 24.7 us -> 22.9 us (0.927)
  Pallas kernels: 23.8 us -> 22 us
    pallas_call x1, Pallas kernels: 23.8 us -> 22 us  [local(): pl.pallas_call(functools.partial(fused, places, inner), out_shape=pltpu.V...]
where the time goes in v3:
time: 22.9 us; the launch traced here: 22.8 us
  Pallas kernels  22 us (96%)
  local copies, waits for them, and re-layouts  0.75 us (3%)
    pallas_call x1, Pallas kernels, local(): pl.pallas_call(functools.partial(fused, places, inner), out_shape=pltpu.V...  22 us
    unnamed x1, local copies, waits for them, and re-layouts  0.75 us

profile of v3, /device:TPU:0, one launch (start us, length us, event | category | flops | bytes accessed | tf_op | source)
XLA Modules:
  0.0 22.8 jit_solution(16990494181890387450)
XLA Ops:
  0.0 22.0 %joint_attention.1 = bf16[128,1536]{1,0:T(8,128)(2,1)S(1)} custom-call(bf16[128,768]{1,0:T(8,128)(2,1)} %queries.1, bf16[128,768]{1,0:T(8,128)(2,1)} %keys.1, bf16[128,768]{1,0:T(8,128)(2,1)} %values.1, bf16[4,768]{1,0:T(4,128)(2,1)} %text_keys.1, bf16[4,768]{1,0:T(4,128)(2,1)} %text_values.1, bf16[4,768]{1,0:T(4,128)(2,1)} %conv_weight.1, ...), custom_call_target="tpu_custom_call" | custom-call | tf_op jit(solution)/shard_map/joint_attention/pallas_call | solution.py:334
  22.0 0.7 %copy.13 = bf16[128,1536]{1,0:T(8,128)(2,1)} copy(bf16[128,1536]{1,0:T(8,128)(2,1)S(1)} %joint_attention.1) | data formatting | bytes 786432

commit v4 on v3

--- a/solution.py
+++ b/solution.py
@@ -11,6 +11,7 @@
 
 HEAD_DIM = 128
 REACH = 1
+PIECES = 2
 MESH = pl.DeviceIdType.MESH
 
 
@@ -179,7 +180,13 @@
     def await_arrival(kind, slot):
         copy_of(kind, slot, 0, at_place(along, across)).wait_recv()
 
-    carried = ((key_buf, key_send, key_recv), (value_buf, value_send, value_recv))
+    pieces = key_send.shape[0]
+    width = features // pieces
+    carried = [
+        (buf.at[:, :, :, piece * width : (piece + 1) * width], send_sem.at[piece], recv_sem.at[piece])
+        for buf, send_sem, recv_sem in ((key_buf, key_send, key_recv), (value_buf, value_send, value_recv))
+        for piece in range(pieces)
+    ]
 
     def send_own():
         for kind in carried:
@@ -245,7 +252,8 @@
         return lambda lanes: buf[at, :, :patches, lanes].reshape(outer * patches, HEAD_DIM)
 
     scores = [scores_with(group_of(key_buf, across))]
-    collect(carried[0])
+    for kind in carried[:pieces]:
+        collect(kind)
     for kind in range(2):
         for place in range(places):
             start = patches + kind * text_rows
@@ -275,7 +283,8 @@
     loads[9].wait()
     loads[10].wait()
 
-    collect(carried[1])
+    for kind in carried[pieces:]:
+        collect(kind)
     for head, lanes in enumerate(lanes_of):
         for number, peer in enumerate(inner_peers):
             summed[head] = summed[head] + jnp.dot(
@@ -355,10 +364,10 @@
             pltpu.VMEM((parts, tokens, width // parts), bf16),
             pltpu.VMEM((parts, tokens, width // parts), bf16),
             sems((11,)),
-            sems((sends,)),
-            sems((inner, outer)),
-            sems((sends,)),
-            sems((inner, outer)),
+            sems((PIECES, sends)),
+            sems((PIECES, inner, outer)),
+            sems((PIECES, sends)),
+            sems((PIECES, inner, outer)),
             sems((parts,)),
             sems((parts,)),
         ],

time: 22.9 us -> 22.3 us (0.974)
  Pallas kernels: 22 us -> 21.4 us
    pallas_call x1, Pallas kernels: 22 us -> 21.4 us  [local(): pl.pallas_call(functools.partial(fused, places, inner), out_shape=pltpu.V...]
where the time goes in v4:
time: 22.3 us; the launch traced here: 22.2 us
  Pallas kernels  21.4 us (96%)
  local copies, waits for them, and re-layouts  0.75 us (3%)
    pallas_call x1, Pallas kernels, local(): pl.pallas_call(functools.partial(fused, places, inner), out_shape=pltpu.V...  21.4 us
    unnamed x1, local copies, waits for them, and re-layouts  0.75 us

profile of v4, /device:TPU:0, one launch (start us, length us, event | category | flops | bytes accessed | tf_op | source)
XLA Modules:
  0.0 22.2 jit_solution(10895545540993986438)
XLA Ops:
  0.0 21.4 %joint_attention.1 = bf16[128,1536]{1,0:T(8,128)(2,1)S(1)} custom-call(bf16[128,768]{1,0:T(8,128)(2,1)} %queries.1, bf16[128,768]{1,0:T(8,128)(2,1)} %keys.1, bf16[128,768]{1,0:T(8,128)(2,1)} %values.1, bf16[4,768]{1,0:T(4,128)(2,1)} %text_keys.1, bf16[4,768]{1,0:T(4,128)(2,1)} %text_values.1, bf16[4,768]{1,0:T(4,128)(2,1)} %conv_weight.1, ...), custom_call_target="tpu_custom_call" | custom-call | tf_op jit(solution)/shard_map/joint_attention/pallas_call | solution.py:343
  21.4 0.7 %copy.13 = bf16[128,1536]{1,0:T(8,128)(2,1)} copy(bf16[128,1536]{1,0:T(8,128)(2,1)S(1)} %joint_attention.1) | data formatting | bytes 786432
